TPU v7x, 32 devices: a whole 2x2x4 slice. The times are simulated.
32 devices in a mesh: group: 2 (over y), tm: 4 (over z), mp: 4 (over x, core).
Axes of the slice: x: 2, y: 2, z: 4, core: 2. Of those that a mesh axis runs over, the one named last changes fastest.
Arguments:
- tokens: bfloat16 [3072, 1536], P(('group', 'tm'), 'mp'), parts along dimension 0, may hold values from -6 to 6
- segment_ids: int32 [3072], P(('group', 'tm')), parts along dimension 0, may hold values from 0 to 7, never falling along the last dimension, each value on 1 to 1152 neighbouring positions
- ln_att_gain: float32 [1536], replicated, may hold values from 0.25 to 1.75
- w_query: bfloat16 [1536, 1536], P(None, 'mp'), may hold values from -3 to 3
- w_keyval: bfloat16 [1536, 2, 1536], P(None, None, 'mp'), may hold values from -0.15625 to 0.15625
- w_out: bfloat16 [1536, 1536], P('mp'), may hold values from -0.21875 to 0.21875
- ln_conv_gain: float32 [1536], replicated, may hold values from 0.25 to 1.75
- w_glu: bfloat16 [1536, 2, 1536], P(None, None, 'mp'), may hold values from -0.15625 to 0.15625
- w_depth: bfloat16 [31, 1536], P(None, 'mp'), may hold values from -1 to 1
- bn_scale: float32 [1536], P('mp'), may hold values from 0.5 to 2
- bn_shift: float32 [1536], P('mp'), may hold values from -3 to 3
- w_proj: bfloat16 [1536, 1536], P('mp'), may hold values from -0.21875 to 0.21875
Outputs:
- block_out: bfloat16 [3072, 1536], P(('group', 'tm'), 'mp'), parts along dimension 0
There are 2 independent parts, one for each index of `group`. A program takes and returns all parts, laid end to end along the dimension named above; an argument that names none is the same for every part. Nothing has to cross between parts.
Inputs may be any that keep to these rules, and one draw needn't show every extreme that they name: `segment_ids`: non-decreasing along the frames; each of the 8 recordings has 1 to 1152 frames and one has exactly that many.
All inputs are finite; a program needn't handle non-finite values.
Results may differ from a plain program's by a relative error of at most 0.015.
The roundings to bfloat16 on the way count: a program that leaves them out, or rounds other values in their place, can miss the bound.
Values may be sent and summed in bfloat16 or wider, within the bound.
A program may use at most 64 MiB of HBM per device.

v0:
```python
import jax
import jax.numpy as jnp
from jax import lax
from jax.sharding import PartitionSpec as P

HEAD_DIM = 96


def with_halo(value, sides, width):
    for axis, dim in sides:
        count, length = (lax.axis_size(axis), value.shape[dim])
        up = [(i, (i + 1) % count) for i in range(count - 1)]
        down = [(j, i) for i, j in up]
        last = lax.slice_in_dim(value, length - width, length, axis=dim)
        initial = lax.slice_in_dim(value, 0, width, axis=dim)
        before = lax.ppermute(last, axis, up)
        after = lax.ppermute(initial, axis, down)
        value = jnp.concatenate([before, value, after], axis=dim)
    return value


def layer_norm(values_in, gain_vec):
    row_mean = jnp.mean(values_in, axis=-1, keepdims=True)
    centered = values_in - row_mean
    spread = jnp.mean(centered * centered, axis=-1, keepdims=True)
    return centered * lax.rsqrt(spread + 1e-05) * gain_vec


def fold_keys(carry_state, query_heads, query_segs, keyval, key_segs, local_cols, score_scale):
    row_max, weight_sum, weighted = carry_state
    key_rows = keyval.shape[0]
    heads_here = query_heads.shape[1]
    key_part = keyval[:, :local_cols].reshape(key_rows, heads_here, -1)
    value_part = keyval[:, local_cols:].reshape(key_rows, heads_here, -1)
    scores = (
        jnp.einsum("qhd,khd->qhk", query_heads, key_part, preferred_element_type=jnp.float32)
        * score_scale
    )
    same_seg = (query_segs[:, None] == key_segs[None, :])[:, None, :]
    scores = jnp.where(same_seg, scores, -jnp.inf)
    new_max = jnp.maximum(row_max, jnp.max(scores, axis=2))
    safe_max = jnp.where(new_max == -jnp.inf, 0.0, new_max)
    weights = jnp.exp(scores - safe_max[:, :, None])
    factor = jnp.exp(row_max - safe_max)
    weight_sum = weight_sum * factor + jnp.sum(weights, axis=2)
    weighted = weighted * factor[:, :, None] + jnp.einsum(
        "qhk,khd->qhd", weights.astype(jnp.bfloat16), value_part, preferred_element_type=jnp.float32
    )
    return (new_max, weight_sum, weighted)


def maybe_fold(carry_state, query_heads, query_segs, keyval, key_segs, local_cols, score_scale):
    return fold_keys(
        carry_state, query_heads, query_segs, keyval, key_segs, local_cols, score_scale
    )


def per_device(
    tokens,
    segment_ids,
    ln_att_gain,
    w_query,
    w_keyval,
    w_out,
    ln_conv_gain,
    w_glu,
    w_depth,
    bn_scale,
    bn_shift,
    w_proj,
):
    row_count = tokens.shape[0]
    full_width = ln_att_gain.shape[0]
    local_cols = w_query.shape[1]
    heads_here = local_cols // HEAD_DIM
    score_scale = HEAD_DIM ** (-0.5)
    all_segs = lax.all_gather(segment_ids, "tm", axis=0, tiled=True)
    anchor = lax.axis_index("tm") * row_count
    whole_rows = lax.all_gather(tokens, "mp", axis=1, tiled=True)
    normed = layer_norm(whole_rows.astype(jnp.float32), ln_att_gain).astype(jnp.bfloat16)
    queries = jnp.dot(normed, w_query, preferred_element_type=jnp.float32).astype(jnp.bfloat16)
    keyval = jnp.dot(
        normed, w_keyval.reshape(full_width, -1), preferred_element_type=jnp.float32
    ).astype(jnp.bfloat16)
    query_heads = queries.reshape(row_count, heads_here, HEAD_DIM)
    initial = (
        jnp.full((row_count, heads_here), -jnp.inf, jnp.float32),
        jnp.zeros((row_count, heads_here), jnp.float32),
        jnp.zeros((row_count, heads_here, HEAD_DIM), jnp.float32),
    )
    segment = lax.all_gather(keyval, "tm", axis=0, tiled=True)
    piece_rows = segment.shape[0]
    block_count = piece_rows // row_count

    def inner_step(state_in, element):
        return (
            maybe_fold(
                state_in, query_heads, segment_ids, element[0], element[1], local_cols, score_scale
            ),
            None,
        )

    stacked = (
        segment.reshape(block_count, row_count, -1),
        all_segs.reshape(block_count, row_count),
    )
    result, unused = lax.scan(inner_step, initial, stacked)
    row_max, weight_sum, weighted = result
    context = (
        (weighted / weight_sum[:, :, None]).reshape(row_count, local_cols).astype(jnp.bfloat16)
    )
    att_terms = jnp.dot(context, w_out, preferred_element_type=jnp.float32)
    att_summed = lax.psum_scatter(
        att_terms.astype(jnp.bfloat16), "mp", scatter_dimension=1, tiled=True
    ).astype(jnp.float32)
    middle = (tokens.astype(jnp.float32) + att_summed).astype(jnp.bfloat16)
    whole_mid = lax.all_gather(middle, "mp", axis=1, tiled=True)
    normed_conv = layer_norm(whole_mid.astype(jnp.float32), ln_conv_gain).astype(jnp.bfloat16)
    both_halves = jnp.dot(
        normed_conv, w_glu.reshape(full_width, -1), preferred_element_type=jnp.float32
    )
    gated = (both_halves[:, :local_cols] * jax.nn.sigmoid(both_halves[:, local_cols:])).astype(
        jnp.bfloat16
    )
    half_width = (w_depth.shape[0] - 1) // 2
    extended = with_halo(gated, (("tm", 0),), half_width).astype(jnp.float32)
    padded_segs = jnp.pad(all_segs, (half_width, half_width), constant_values=-1)
    window_segs = lax.dynamic_slice_in_dim(padded_segs, anchor, row_count + 2 * half_width, 0)
    depth = jnp.zeros((row_count, local_cols), jnp.float32)
    for tap_index in range(w_depth.shape[0]):
        same_seg = (window_segs[tap_index : tap_index + row_count] == segment_ids)[:, None]
        shifted = jnp.where(same_seg, extended[tap_index : tap_index + row_count], 0.0)
        depth = depth + shifted * w_depth[tap_index].astype(jnp.float32)
    normalized = depth * bn_scale + bn_shift
    swished = (normalized * jax.nn.sigmoid(normalized)).astype(jnp.bfloat16)
    conv_terms = jnp.dot(swished, w_proj, preferred_element_type=jnp.float32)
    conv_summed = lax.psum_scatter(
        conv_terms.astype(jnp.bfloat16), "mp", scatter_dimension=1, tiled=True
    ).astype(jnp.float32)
    return (middle.astype(jnp.float32) + conv_summed).astype(jnp.bfloat16)


def solution(mesh):
    placed = (
        P(("group", "tm"), "mp"),
        P(("group", "tm")),
        P(),
        P(None, "mp"),
        P(None, None, "mp"),
        P("mp", None),
        P(),
        P(None, None, "mp"),
        P(None, "mp"),
        P("mp"),
        P("mp"),
        P("mp", None),
    )
    return jax.shard_map(
        per_device, mesh=mesh, in_specs=placed, out_specs=P(("group", "tm"), "mp"), check_vma=False
    )
```

profile of v0, /device:TPU:8, one launch (start us, length us, event | category | flops | bytes accessed | tf_op | source)
XLA Modules:
  0.0 227.5 jit_solution(7749308637587739135)
XLA Ops:
  7.3 3.5 %copy.24 = bf16[192,8,2,384]{3,1,2,0:T(8,128)(2,1)} copy(bf16[192,8,2,384]{3,2,1,0:T(2,128)(2,1)} %bitcast.66) | data formatting | bytes 4718592
  10.9 16.7 %all-gather.5.cloned.1.call-done = bf16[384,1536]{1,0:T(8,128)(2,1)} async-done(((bf16[384,384]{1,0:T(8,128)(2,1)}), bf16[384,1536]{1,0:T(8,128)(2,1)}) %all-gather.5.cloned.1.call-update) | async-done | bytes 1179664 | tf_op jit(solution)/shard_map/all_gather | solution.py:79
  29.2 1.7 fusion.19
  30.9 3.6 %convolution_convert_fusion.2 = bf16[384,768]{1,0:T(8,128)(2,1)} fusion(bf16[1536,768]{1,0:T(8,128)(2,1)} %bitcast.69, bf16[384,1536]{1,0:T(8,128)(2,1)S(1)} %copy-done.4, f32[1536]{0:T(1024)S(1)} %copy-done.15, f32[384]{0:T(512)S(1)} %add_rsqrt_fusion.1, f32[384]{0:T(512)S(1)} %broadcast_multiply_fusion.1), kind=kOutput, calls=%fused_computation.38 | convolution fusion | flops 909213696 | bytes 4137984 | tf_op jit(solution)/shard_map/dot_general | solution.py:82
  35.3 11.9 %all-gather = s32[4,1,384]{2,1,0:T(1,128)S(1)} all-gather(s32[1,1,384]{2,1,0:T(1,128)S(1)} %reshape.145), channel_id=1, replica_groups=mesh['group'=2,'tm'=4,'mp'=4] {'tm'}, dimensions={0}, use_global_device_ids=true | all-gather | bytes 7680 | tf_op jit(solution)/shard_map/all_gather | solution.py:77
  47.8 2.9 %convolution_convert_fusion.3 = bf16[384,384]{0,1:T(8,128)(2,1)} fusion(bf16[1536,384]{1,0:T(8,128)(2,1)} %param.17, bf16[384,1536]{1,0:T(8,128)(2,1)S(1)} %copy-done.4, f32[1536]{0:T(1024)S(1)} %copy-done.15, f32[384]{0:T(512)S(1)} %add_rsqrt_fusion.1, f32[384]{0:T(512)S(1)} %broadcast_multiply_fusion.1), kind=kOutput, calls=%fused_computation.39 | convolution fusion | flops 456081408 | bytes 2663424 | tf_op jit(solution)/shard_map/dot_general | solution.py:81
  50.8 32.9 %all-gather.7.cloned.1.call-done = bf16[1536,768]{1,0:T(8,128)(2,1)} async-done(((bf16[384,768]{1,0:T(8,128)(2,1)}), bf16[1536,768]{1,0:T(8,128)(2,1)}) %all-gather.7.cloned.1.call-update) | async-done | bytes 2359312 | tf_op jit(solution)/shard_map/all_gather | solution.py:91
  83.6 37.2 %while.15 = (s32[]{:T(128)}, f32[384,4]{0,1:T(4,128)S(1)}, f32[384,4]{0,1:T(4,128)}, f32[384,4,96]{0,2,1:T(8,128)}, s32[384]{0:T(512)}, /*index=5*/s32[4,384]{1,...) while((s32[]{:T(128)}, f32[384,4]{0,1:T(4,128)S(1)}, ...), condition=%wide.region_5.6_spmd.clone, body=%wide.region_2.5_spmd.clone.sunk | while | flops 233584128 | bytes 19919136 | solution.py:107
  88.0 1.6 fusion.124
  97.3 1.6 fusion.124
  106.6 1.6 fusion.124
  115.9 1.6 fusion.124
  124.2 26.2 %reduce-scatter.7.cloned.1.call-done = bf16[384,384]{1,0:T(8,128)(2,1)} async-done(((bf16[1536,384]{1,0:T(8,128)(2,1)}), bf16[384,384]{1,0:T(8,128)(2,1)}) %reduce-scatter.7.cloned.1.call-update) | async-done | bytes 294928
  150.5 1.8 copy.19
  152.3 1.8 add_convert_fusion.1
  154.3 1.9 copy.25
  158.9 12.9 %all-gather.9.cloned.1.call-done = bf16[384,1536]{1,0:T(8,128)(2,1)} async-done(((bf16[384,384]{1,0:T(8,128)(2,1)}), bf16[384,1536]{1,0:T(8,128)(2,1)}) %all-gather.9.cloned.1.call-update) | async-done | bytes 1179664 | tf_op jit(solution)/shard_map/all_gather | solution.py:117
  173.4 1.7 fusion.16
  175.2 2.8 %fusion.22 = f32[384,768]{1,0:T(8,128)S(1)} fusion(bf16[1536,768]{1,0:T(8,128)(2,1)} %bitcast.68, bf16[384,1536]{1,0:T(8,128)(2,1)S(1)} %copy-done.3, f32[1536]{0:T(1024)S(1)} %copy-done.16, f32[384]{0:T(512)S(1)} %add_rsqrt_fusion, f32[384]{0:T(512)S(1)} %broadcast_multiply_fusion), kind=kOutput, calls=%fused_computation.40 | convolution fusion | flops 908918784 | bytes 4727808 | tf_op jit(solution)/shard_map/dot_general | solution.py:119
  178.2 3.5 %collective-permute-start = (bf16[15,384]{1,0:T(8,128)(2,1)S(1)}, bf16[15,384]{1,0:T(8,128)(2,1)S(1)}, u32[]{:S(2)}, u32[]{:S(2)}) collective-permute-start(bf16[15,384]{1,0:T(8,128)(2,1)S(1)} %get-tuple-element.148), channel_id=1, source_target_pairs={{0,4},{4,8},{8,12},{1,5},{5,9},{9,13},{2,6},{6,10},{10,14},{3,7},{... | collective-permute-start | bytes 34568 | tf_op jit(solution)/shard_map/ppermute | solution.py:16
  181.8 2.6 %collective-permute-start.1 = (bf16[15,384]{1,0:T(8,128)(2,1)S(1)}, bf16[15,384]{1,0:T(8,128)(2,1)S(1)}, u32[]{:S(2)}, u32[]{:S(2)}) collective-permute-start(bf16[15,384]{1,0:T(8,128)(2,1)S(1)} %get-tuple-element.149), channel_id=1, source_target_pairs={{4,0},{8,4},{12,8},{5,1},{9,5},{13,9},{6,2},{10,6},{14,10},{7,3},{... | collective-permute-start | bytes 34568 | tf_op jit(solution)/shard_map/ppermute | solution.py:17
  184.5 2.9 %collective-permute-done.1 = bf16[15,384]{1,0:T(8,128)(2,1)S(1)} collective-permute-done((bf16[15,384]{1,0:T(8,128)(2,1)S(1)}, bf16[15,384]{1,0:T(8,128)(2,1)S(1)}, u32[]{:S(2)}, u32[]{:S(2)}) %collective-permute-start.1) | collective-permute-done | bytes 11552 | tf_op jit(solution)/shard_map/ppermute | solution.py:17
  187.5 5.1 %convolution_convert_fusion = bf16[384,1536]{1,0:T(8,128)(2,1)S(1)} fusion(bf16[384,1536]{1,0:T(8,128)(2,1)S(1)} %copy-done.14, f32[414,384]{1,0:T(8,128)S(1)} %maximum_convert_fusion, f32[384]{0:T(512)S(1)} %copy-done.17, f32[384]{0:T(512)S(1)} %copy-done.18, f32[384]{0:T(512)S(1)} %get-tuple-element.122, f32[384]{0:T(512)S(1)} %get-tuple-element.123, ...), kind=kOutput, calls=%fused_computation.30 | convolution fusion | flops 468172800 | bytes 20727296 | tf_op jit(solution)/shard_map/dot_general | solution.py:136
  194.1 24.9 %reduce-scatter.9.cloned.1.call-done = bf16[384,384]{1,0:T(8,128)(2,1)} async-done(((bf16[1536,384]{1,0:T(8,128)(2,1)}), bf16[384,384]{1,0:T(8,128)(2,1)}) %reduce-scatter.9.cloned.1.call-update) | async-done | bytes 294928
  (152 shorter events, 45.6 us)
Async XLA Ops:
  6.5 115.4 %copy-start = (bf16[384,1536]{1,0:T(8,128)(2,1)S(1)}, bf16[384,1536]{1,0:T(8,128)(2,1)}, u32[]{:S(2)}) copy-start(bf16[384,1536]{1,0:T(8,128)(2,1)} %param.19) | copy-start | bytes 3538948
  6.5 21.0 %all-gather.5.cloned.1.call-start = ((), (), s32[]{:S(2)}) async-start(), calls=%async_computation.2 | async-start | bytes 1474560 | tf_op jit(solution)/shard_map/all_gather | solution.py:79
  7.3 76.4 %all-gather.7.cloned.1.call-start = ((), (), s32[]{:S(2)}) async-start(), calls=%async_computation.3 | async-start | bytes 2949120 | tf_op jit(solution)/shard_map/all_gather | solution.py:91
  10.9 20.0 %copy-start.15 = (f32[1536]{0:T(1024)S(1)}, f32[1536]{0:T(1024)}, u32[]{:S(2)}) copy-start(f32[1536]{0:T(1024)} %param.16) | copy-start | bytes 18436
  27.6 3.3 %copy-start.4 = (bf16[384,1536]{1,0:T(8,128)(2,1)S(1)}, bf16[384,1536]{1,0:T(8,128)(2,1)}, u32[]{:S(2)}) copy-start(bf16[384,1536]{1,0:T(8,128)(2,1)} %all-gather.5.cloned.1.call-done) | copy-start | bytes 3538948
  34.6 115.9 %reduce-scatter.7.cloned.1.call-start = ((), (), s32[]{:S(2)}) async-start(), calls=%async_computation.5 | async-start | bytes 1474560
  47.2 36.4 %copy-start.12 = (s32[4,1,384]{2,1,0:T(1,128)}, s32[4,1,384]{2,1,0:T(1,128)S(1)}, u32[]{:S(2)}) copy-start(s32[4,1,384]{2,1,0:T(1,128)S(1)} %all-gather) | copy-start | bytes 18436
  91.2 1.7 copy-start.10
  100.5 1.7 copy-start.10
  109.8 1.7 copy-start.10
  119.1 1.7 copy-start.10
  122.8 31.5 %copy-start.13 = (s32[4,1,384]{2,1,0:T(1,128)S(1)}, s32[4,1,384]{2,1,0:T(1,128)}, u32[]{:S(2)}) copy-start(s32[4,1,384]{2,1,0:T(1,128)} %copy-done.12) | copy-start | bytes 18436
  124.2 30.1 %copy-start.6 = (bf16[1536,2,384]{2,1,0:T(2,128)(2,1)S(1)}, bf16[1536,2,384]{2,1,0:T(2,128)(2,1)}, u32[]{:S(2)}) copy-start(bf16[1536,2,384]{2,1,0:T(2,128)(2,1)} %param.21) | copy-start | bytes 7077892
  124.2 47.6 %all-gather.9.cloned.1.call-start = ((), (), s32[]{:S(2)}) async-start(), calls=%async_computation.4 | async-start | bytes 1474560 | tf_op jit(solution)/shard_map/all_gather | solution.py:117
  154.2 64.8 %reduce-scatter.9.cloned.1.call-start = ((), (), s32[]{:S(2)}) async-start(), calls=%async_computation.6 | async-start | bytes 1474560
  156.2 18.9 %copy-start.16 = (f32[1536]{0:T(1024)S(1)}, f32[1536]{0:T(1024)}, u32[]{:S(2)}) copy-start(f32[1536]{0:T(1024)} %param.20) | copy-start | bytes 18436
  171.8 3.3 %copy-start.3 = (bf16[384,1536]{1,0:T(8,128)(2,1)S(1)}, bf16[384,1536]{1,0:T(8,128)(2,1)}, u32[]{:S(2)}) copy-start(bf16[384,1536]{1,0:T(8,128)(2,1)} %all-gather.9.cloned.1.call-done) | copy-start | bytes 3538948
  175.2 9.3 %copy-start.11 = (bf16[31,384]{1,0:T(8,128)(2,1)S(1)}, bf16[31,384]{1,0:T(8,128)(2,1)}, u32[]{:S(2)}) copy-start(bf16[31,384]{1,0:T(8,128)(2,1)} %param.22) | copy-start | bytes 71428
  178.0 9.4 %copy-start.14 = (bf16[384,1536]{1,0:T(8,128)(2,1)S(1)}, bf16[384,1536]{1,0:T(8,128)(2,1)}, u32[]{:S(2)}) copy-start(bf16[384,1536]{1,0:T(8,128)(2,1)} %param.25) | copy-start | bytes 3538948
  178.0 9.4 %copy-start.17 = (f32[384]{0:T(512)S(1)}, f32[384]{0:T(512)}, u32[]{:S(2)}) copy-start(f32[384]{0:T(512)} %param.24) | copy-start | bytes 4612
  178.0 9.4 %copy-start.18 = (f32[384]{0:T(512)S(1)}, f32[384]{0:T(512)}, u32[]{:S(2)}) copy-start(f32[384]{0:T(512)} %param.23) | copy-start | bytes 4612
  178.2 6.2 %collective-permute-start = (bf16[15,384]{1,0:T(8,128)(2,1)S(1)}, bf16[15,384]{1,0:T(8,128)(2,1)S(1)}, u32[]{:S(2)}, u32[]{:S(2)}) collective-permute-start(bf16[15,384]{1,0:T(8,128)(2,1)S(1)} %get-tuple-element.148), channel_id=1, source_target_pairs={{0,4},{4,8},{8,12},{1,5},{5,9},{9,13},{2,6},{6,10},{10,14},{3,7},{... | collective-permute-start | bytes 34568 | tf_op jit(solution)/shard_map/ppermute | solution.py:16
  181.8 5.6 %collective-permute-start.1 = (bf16[15,384]{1,0:T(8,128)(2,1)S(1)}, bf16[15,384]{1,0:T(8,128)(2,1)S(1)}, u32[]{:S(2)}, u32[]{:S(2)}) collective-permute-start(bf16[15,384]{1,0:T(8,128)(2,1)S(1)} %get-tuple-element.149), channel_id=1, source_target_pairs={{4,0},{8,4},{12,8},{5,1},{9,5},{13,9},{6,2},{10,6},{14,10},{7,3},{... | collective-permute-start | bytes 34568 | tf_op jit(solution)/shard_map/ppermute | solution.py:17
  192.6 27.6 %copy-start.5 = (bf16[384,384]{1,0:T(8,128)(2,1)S(1)}, bf16[384,384]{1,0:T(8,128)(2,1)}, u32[]{:S(2)}) copy-start(bf16[384,384]{1,0:T(8,128)(2,1)} %add_convert_fusion.1) | copy-start | bytes 884740
  (20 other events, 28.8 us)
Sparse Core Ops, SparseCore 0:
  8.9 18.5 all-gather.4
  34.7 48.8 all-gather.6
  124.3 26.1 reduce-scatter.6
  154.3 17.4 all-gather.8
  194.2 24.7 reduce-scatter.8
where the time goes:
time: 230 us; the launch traced here: 227 us
  waiting for transfers between devices  117 us (51%)
  local copies, waits for them, and re-layouts  27.7 us (12%)
  other arithmetic  25.4 us (11%)
  matrix products  25 us (11%)
  between operations  13.4 us (6%)
  blocking collectives  11.9 us (5%)
  starting transfers between devices  6.32 us (3%)
    unnamed x7, waiting for transfers between devices  52 us
    all_gather x1, waiting for transfers between devices, per_device(): segment = lax.all_gather(keyval, 'tm', axis=0, tiled=True)  32.9 us
    all_gather x1, waiting for transfers between devices, per_device(): whole_rows = lax.all_gather(tokens, 'mp', axis=1, tiled=True)  16.7 us
    all_gather x1, waiting for transfers between devices, per_device(): whole_mid = lax.all_gather(middle, 'mp', axis=1, tiled=True)  12.9 us
    unnamed x35, local copies, waits for them, and re-layouts  12.6 us
    all_gather x1, blocking collectives, per_device(): all_segs = lax.all_gather(segment_ids, 'tm', axis=0, tiled=True)  11.9 us
    dynamic_slice x12, local copies, waits for them, and re-layouts, per_device(): result, unused = lax.scan(inner_step, initial, stacked)  8.47 us
    dot_general x4, matrix products, fold_keys(): jnp.einsum('qhd,khd->qhk', query_heads, key_part, preferred_element_type=...  6.41 us
  transfers between devices with their start and end apart: 7, of which 6 were waited for; matrix products, arithmetic and copies ran while one was open for 5% of the time, Pallas kernels for 0%

commit v1 on v0

--- a/solution.py
+++ b/solution.py
@@ -1,6 +1,10 @@
+import functools
+
 import jax
 import jax.numpy as jnp
 from jax import lax
+from jax.experimental import pallas as pl
+from jax.experimental.pallas import tpu as pltpu
 from jax.sharding import PartitionSpec as P
 
 HEAD_DIM = 96
@@ -140,6 +144,435 @@
     return (middle.astype(jnp.float32) + conv_summed).astype(jnp.bfloat16)
 
 
+NEG = -1e30
+HALO = 16
+NCH = 2
+MESH = pl.DeviceIdType.MESH
+F32 = jnp.float32
+BF16 = jnp.bfloat16
+
+
+def block_kernel(
+    T, taps,
+    tokens, segrow, segcol, g_att, wq_h, wkv_h, wo_h, g_conv, wg_h, wdep, bns, bnb, wp_h,
+    out,
+    tok, seg_all, seg_ext, wq, wkv, wo, wg, wp, nrm, kbuf, qm, vm, sc, pw, mst, lst, acc,
+    ctx, keep, mid, ext, wdf, sa, sx, sb, ra, rx, rb,
+    wsem, tok_recv, z_send, x_send, m_send, seg_send, seg_recv, hs_send, hs_recv,
+    hg_send, hg_recv, rs_send, rs_recv, mid_send, mid_recv,
+):
+    R, C = tokens.shape
+    M = 4
+    D = M * C
+    heads = C // HEAD_DIM
+    CR = R // NCH
+    t = lax.axis_index("tm")
+    m = lax.axis_index("mp")
+    mate = m + 1 - 2 * (m % 2)
+    cross = (m + 2) % 4
+    diag = (mate + 2) % 4
+
+    def rcopy(src, dst, ssem, rsem, **dev):
+        return pltpu.make_async_remote_copy(
+            src_ref=src, dst_ref=dst, send_sem=ssem, recv_sem=rsem,
+            device_id=dev, device_id_type=MESH,
+        )
+
+    loads = [
+        pltpu.make_async_copy(wq_h, wq, wsem.at[0]),
+        pltpu.make_async_copy(wkv_h, wkv, wsem.at[1]),
+        pltpu.make_async_copy(wg_h, wg, wsem.at[2]),
+    ]
+    for b in range(M):
+        cols = pl.ds(b * C, C)
+        loads.append(pltpu.make_async_copy(wo_h.at[:, cols], wo.at[b], wsem.at[3 + b]))
+        loads.append(pltpu.make_async_copy(wp_h.at[:, cols], wp.at[b], wsem.at[7 + b]))
+    for c in loads:
+        c.start()
+
+    barrier = pltpu.get_barrier_semaphore()
+    for peer in (mate, cross):
+        pl.semaphore_signal(barrier, inc=1, device_id={"mp": peer}, device_id_type=MESH)
+    for d in range(1, T):
+        pl.semaphore_signal(
+            barrier, inc=1, device_id={"tm": (t + d) % T}, device_id_type=MESH
+        )
+    tok[t, m] = tokens[...]
+    seg_all[t] = segrow[...]
+    seg_ext[0, pl.ds(HALO, R), :] = segcol[...]
+    pl.semaphore_wait(barrier, 1 + T)
+
+    def z_right(s):
+        return rcopy(tok.at[s, m], tok.at[s, m], z_send.at[0, s], tok_recv.at[s, m],
+                     tm=(t + 1) % T)
+
+    def z_left(s):
+        return rcopy(tok.at[s, m], tok.at[s, m], z_send.at[1, s], tok_recv.at[s, m],
+                     tm=(t + T - 1) % T)
+
+    def over_x(s, col):
+        return rcopy(tok.at[s, col], tok.at[s, col], x_send.at[s], tok_recv.at[s, col],
+                     mp=cross)
+
+    def to_mate(s, col, k):
+        return rcopy(tok.at[s, col], tok.at[s, col], m_send.at[s, k], tok_recv.at[s, col],
+                     mp=mate)
+
+    def launch(s):
+        @pl.when(jnp.logical_and(s <= t, t < T - 1))
+        def _():
+            z_right(s).start()
+
+        @pl.when(jnp.logical_and(s >= t, t > 0))
+        def _():
+            z_left(s).start()
+
+        over_x(s, m).start()
+        to_mate(s, m, 0).start()
+
+    launch(t)
+
+    def seg_copy(d):
+        return rcopy(seg_all.at[t], seg_all.at[t], seg_send.at[d], seg_recv.at[t],
+                     tm=(t + d) % T)
+
+    for d in range(1, T):
+        seg_copy(d).start()
+
+    def halo_right(ref, ssem, rsem):
+        return rcopy(ref.at[:, pl.ds(R, HALO)], ref.at[:, pl.ds(0, HALO)], ssem.at[0],
+                     rsem.at[0], tm=(t + 1) % T)
+
+    def halo_left(ref, ssem, rsem):
+        return rcopy(ref.at[:, pl.ds(HALO, HALO)], ref.at[:, pl.ds(R + HALO, HALO)],
+                     ssem.at[1], rsem.at[1], tm=(t + T - 1) % T)
+
+    has_right = t < T - 1
+    has_left = t > 0
+
+    @pl.when(has_right)
+    def _():
+        halo_right(seg_ext, hs_send, hs_recv).start()
+
+    @pl.when(has_left)
+    def _():
+        halo_left(seg_ext, hs_send, hs_recv).start()
+
+    @pl.when(jnp.logical_not(has_left))
+    def _():
+        seg_ext[0, pl.ds(0, HALO), :] = jnp.full((HALO, 128), -1, jnp.int32)
+        ext[:, pl.ds(0, HALO), :] = jnp.zeros((C // 128, HALO, 128), F32)
+
+    @pl.when(jnp.logical_not(has_right))
+    def _():
+        seg_ext[0, pl.ds(R + HALO, HALO), :] = jnp.full((HALO, 128), -1, jnp.int32)
+        ext[:, pl.ds(R + HALO, HALO), :] = jnp.zeros((C // 128, HALO, 128), F32)
+
+    wdf[pl.ds(0, taps), :] = wdep[...].astype(F32)
+    mst[...] = jnp.full(mst.shape, NEG, F32)
+    lst[...] = jnp.zeros(lst.shape, F32)
+    acc[...] = jnp.zeros(acc.shape, F32)
+    head_of = lax.broadcasted_iota(jnp.int32, (1, C), 1) // HEAD_DIM
+
+    def norm_rows(load, gain, r0, n):
+        parts = [load(b, r0, n).astype(F32) for b in range(M)]
+        total = parts[0] + parts[1] + parts[2] + parts[3]
+        mean = jnp.sum(total, axis=1, keepdims=True) * (1.0 / D)
+        parts = [p - mean for p in parts]
+        sq = parts[0] * parts[0]
+        for p in parts[1:]:
+            sq = sq + p * p
+        inv = lax.rsqrt(jnp.sum(sq, axis=1, keepdims=True) * (1.0 / D) + 1e-05)
+        for b in range(M):
+            nrm[pl.ds(r0, n), pl.ds(b * C, C)] = (
+                parts[b] * inv * gain[:, pl.ds(b * C, C)]
+            ).astype(BF16)
+
+    RT = 32
+    coef = float(HEAD_DIM ** (-0.5) * 1.4426950408889634)
+
+    def softmax_rows(s, rt):
+        r0 = pl.multiple_of(rt * RT, RT)
+        rows = pl.ds(r0, RT)
+        same = segcol[rows, pl.ds(0, 1)] == seg_all[s, pl.ds(0, 1), :]
+        bias = jnp.where(same, 0.0, NEG)
+        lanes = None
+        for h in range(heads):
+            x = sc[pl.ds(pl.multiple_of(h * R + r0, RT), RT), :] + bias
+            old = mst[h, rows, :]
+            new = jnp.maximum(old, jnp.max(x, axis=1, keepdims=True))
+            f = jnp.exp2((old - new) * coef)
+            p = jnp.exp2((x - new[:, :1]) * coef)
+            lst[h, rows, :] = lst[h, rows, :] * f + jnp.sum(p, axis=1, keepdims=True)
+            mst[h, rows, :] = new
+            pw[rows, pl.ds(h * R, R)] = p.astype(BF16)
+            wide = jnp.broadcast_to(f[:, :1], (RT, C))
+            lanes = wide if lanes is None else jnp.where(head_of == h, wide, lanes)
+        acc[rows, :] = acc[rows, :] * lanes
+
+    def block_step(i, code):
+        s = code % T
+        nxt = (code // T) % T
+
+        @pl.when(i + 1 < T)
+        def _():
+            z_right(nxt).wait_recv()
+            launch(nxt)
+
+        over_x(s, cross).wait_recv()
+        to_mate(s, cross, 1).start()
+        to_mate(s, mate, 0).wait_recv()
+        to_mate(s, diag, 1).wait_recv()
+
+        @pl.when(i == 0)
+        def _():
+            loads[0].wait()
+            loads[1].wait()
+
+        @pl.when(i > 0)
+        def _():
+            rcopy(seg_all.at[s], seg_all.at[s], seg_send.at[0], seg_recv.at[s],
+                  tm=(t + 1) % T).wait_recv()
+
+        @pl.loop(0, R // RT)
+        def _(rt):
+            norm_rows(lambda b, r0, n: tok[s, b, pl.ds(r0, n), :], g_att,
+                      pl.multiple_of(rt * RT, RT), RT)
+
+        @pl.when(i == 0)
+        def _():
+            q = jnp.dot(nrm[...], wq[...], preferred_element_type=F32).astype(BF16)
+            for h in range(heads):
+                qm[pl.ds(h * R, R), :] = jnp.where(head_of == h, q, jnp.zeros_like(q))
+
+        kbuf[...] = jnp.dot(
+            nrm[...], wkv[:, pl.ds(0, C)], preferred_element_type=F32).astype(BF16)
+        v = jnp.dot(nrm[...], wkv[:, pl.ds(C, C)], preferred_element_type=F32).astype(BF16)
+        for h in range(heads):
+            vm[pl.ds(h * R, R), :] = jnp.where(head_of == h, v, jnp.zeros_like(v))
+        for h in range(heads):
+            sc[pl.ds(h * R, R), :] = lax.dot_general(
+                qm[pl.ds(h * R, R), :], kbuf[...], (((1,), (1,)), ((), ())),
+                preferred_element_type=F32)
+
+        @pl.loop(0, R // RT)
+        def _(rt):
+            softmax_rows(s, rt)
+
+        acc[...] += jnp.dot(pw[...], vm[...], preferred_element_type=F32)
+        return code // T
+
+    order = 228 - 3 * ((t + 3) // 4) - 171 * ((t + 2) // 4) - 27 * ((t + 1) // 4)
+    lax.fori_loop(0, T, block_step, order)
+
+    den = None
+    for h in range(heads):
+        wide = jnp.broadcast_to(lst[h, :, pl.ds(0, 1)], (R, C))
+        den = wide if den is None else jnp.where(head_of == h, wide, den)
+    ctx[...] = (acc[...] / den).astype(BF16)
+
+    def rs_a(ph, ch):
+        return rcopy(sa.at[ph, ch], ra.at[ph, ch], rs_send.at[ph, ch, 0],
+                     rs_recv.at[ph, ch, 0], mp=mate)
+
+    def rs_x(ph, ch):
+        return rcopy(sx.at[ph, ch], rx.at[ph, ch], rs_send.at[ph, ch, 1],
+                     rs_recv.at[ph, ch, 1], mp=cross)
+
+    def rs_b(ph, ch):
+        return rcopy(sb.at[ph, ch], rb.at[ph, ch], rs_send.at[ph, ch, 2],
+                     rs_recv.at[ph, ch, 2], mp=mate)
+
+    def scatter_chunk(ph, w, ch):
+        a = ctx[pl.ds(ch * CR, CR), :]
+        sa[ph, ch] = jnp.dot(a, w[diag], preferred_element_type=F32).astype(BF16)
+        rs_a(ph, ch).start()
+        mine = jnp.dot(a, w[cross], preferred_element_type=F32)
+        sb[ph, ch] = jnp.dot(a, w[mate], preferred_element_type=F32).astype(BF16)
+        rs_b(ph, ch).start()
+        rs_a(ph, ch).wait_recv()
+        sx[ph, ch] = (mine + ra[ph, ch].astype(F32)).astype(BF16)
+        rs_x(ph, ch).start()
+        keep[pl.ds(ch * CR, CR), :] = (
+            jnp.dot(a, w[m], preferred_element_type=F32).astype(BF16).astype(F32))
+
+    def summed(ph, ch):
+        rs_b(ph, ch).wait_recv()
+        rs_x(ph, ch).wait_recv()
+        return (keep[pl.ds(ch * CR, CR), :] + rb[ph, ch].astype(F32)) + rx[ph, ch].astype(F32)
+
+    for b in range(M):
+        loads[3 + 2 * b].wait()
+    for ch in range(NCH):
+        scatter_chunk(0, wo, ch)
+
+    def mid_copy(col, ch, k, **dev):
+        piece = mid.at[col, pl.ds(ch * CR, CR)]
+        return rcopy(piece, piece, mid_send.at[ch, k], mid_recv.at[col, ch], **dev)
+
+    for ch in range(NCH):
+        rows = pl.ds(ch * CR, CR)
+        mid[m, rows, :] = (tokens[rows, :].astype(F32) + summed(0, ch)).astype(BF16)
+        mid_copy(m, ch, 0, mp=cross).start()
+        mid_copy(m, ch, 1, mp=mate).start()
+    loads[2].wait()
+    for ch in range(NCH):
+        rows = pl.ds(ch * CR, CR)
+        mid_copy(cross, ch, 0, mp=cross).wait_recv()
+        mid_copy(cross, ch, 2, mp=mate).start()
+        mid_copy(mate, ch, 1, mp=mate).wait_recv()
+        mid_copy(diag, ch, 2, mp=mate).wait_recv()
+
+        @pl.loop(0, CR // RT)
+        def _(rt):
+            norm_rows(lambda b, r0, n: mid[b, pl.ds(r0, n), :], g_conv,
+                      pl.multiple_of(ch * CR + rt * RT, RT), RT)
+
+        a = nrm[rows, :]
+        val = jnp.dot(a, wg[:, pl.ds(0, C)], preferred_element_type=F32)
+        gate = jnp.dot(a, wg[:, pl.ds(C, C)], preferred_element_type=F32)
+        gated = (val * jax.nn.sigmoid(gate)).astype(BF16).astype(F32)
+        for k in range(C // 128):
+            ext[k, pl.ds(HALO + ch * CR, CR), :] = gated[:, k * 128:(k + 1) * 128]
+        if ch == 0:
+            @pl.when(has_left)
+            def _():
+                halo_left(ext, hg_send, hg_recv).start()
+
+    @pl.when(has_right)
+    def _():
+        halo_right(ext, hg_send, hg_recv).start()
+
+    @pl.when(has_left)
+    def _():
+        halo_right(seg_ext, hs_send, hs_recv).wait_recv()
+        halo_right(ext, hg_send, hg_recv).wait_recv()
+
+    @pl.when(has_right)
+    def _():
+        halo_left(seg_ext, hs_send, hs_recv).wait_recv()
+        halo_left(ext, hg_send, hg_recv).wait_recv()
+
+    half = (taps - 1) // 2
+    for b in range(M):
+        loads[4 + 2 * b].wait()
+    for ch in range(NCH):
+        @pl.loop(0, CR // RT)
+        def _(rt):
+            r0 = pl.multiple_of(ch * CR + rt * RT, RT)
+            here = segcol[pl.ds(r0, RT), :]
+            groups = [pl.ds(k * 128, 128) for k in range(C // 128)]
+            depth = [jnp.zeros((RT, 128), F32) for _ in groups]
+            for j in range(taps):
+                at = pl.ds(r0 + (j + HALO - half), RT)
+                same = seg_ext[0, at, :] == here
+                for k, g in enumerate(groups):
+                    depth[k] += jnp.where(same, ext[k, at, :], 0.0) * wdf[pl.ds(j, 1), g]
+            for k, g in enumerate(groups):
+                z = depth[k] * bns[:, g] + bnb[:, g]
+                ctx[pl.ds(r0, RT), g] = (z * jax.nn.sigmoid(z)).astype(BF16)
+
+        scatter_chunk(1, wp, ch)
+    for ch in range(NCH):
+        rows = pl.ds(ch * CR, CR)
+        out[rows, :] = (mid[m, rows, :].astype(F32) + summed(1, ch)).astype(BF16)
+
+    for s in range(T):
+        @pl.when(jnp.logical_and(s <= t, t < T - 1))
+        def _():
+            z_right(s).wait_send()
+
+        @pl.when(jnp.logical_and(s >= t, t > 0))
+        def _():
+            z_left(s).wait_send()
+
+        over_x(s, m).wait_send()
+        to_mate(s, m, 0).wait_send()
+        to_mate(s, cross, 1).wait_send()
+    for d in range(1, T):
+        seg_copy(d).wait_send()
+
+    @pl.when(has_right)
+    def _():
+        halo_right(seg_ext, hs_send, hs_recv).wait_send()
+        halo_right(ext, hg_send, hg_recv).wait_send()
+
+    @pl.when(has_left)
+    def _():
+        halo_left(seg_ext, hs_send, hs_recv).wait_send()
+        halo_left(ext, hg_send, hg_recv).wait_send()
+
+    for ch in range(NCH):
+        for ph in range(2):
+            rs_a(ph, ch).wait_send()
+            rs_x(ph, ch).wait_send()
+            rs_b(ph, ch).wait_send()
+        mid_copy(m, ch, 0, mp=cross).wait_send()
+        mid_copy(m, ch, 1, mp=mate).wait_send()
+        mid_copy(cross, ch, 2, mp=mate).wait_send()
+
+
+def fused_device(
+    tokens, segment_ids, ln_att_gain, w_query, w_keyval, w_out, ln_conv_gain, w_glu,
+    w_depth, bn_scale, bn_shift, w_proj,
+):
+    R, C = tokens.shape
+    D = ln_att_gain.shape[0]
+    T = lax.axis_size("tm")
+    M = D // C
+    heads = C // HEAD_DIM
+    taps = w_depth.shape[0]
+    CR = R // NCH
+    segrow = jnp.broadcast_to(segment_ids[None, :], (8, R))
+    segcol = jnp.broadcast_to(segment_ids[:, None], (R, 128))
+    vmem = pl.BlockSpec(memory_space=pltpu.VMEM)
+    hbm = pl.BlockSpec(memory_space=pl.ANY)
+    dma = pltpu.SemaphoreType.DMA
+    part = pltpu.VMEM((2, NCH, CR, C), BF16)
+    return pl.pallas_call(
+        functools.partial(block_kernel, T, taps),
+        out_shape=jax.ShapeDtypeStruct((R, C), BF16),
+        in_specs=[vmem, vmem, vmem, vmem, hbm, hbm, hbm, vmem, hbm, vmem, vmem, vmem, hbm],
+        out_specs=vmem,
+        scratch_shapes=[
+            pltpu.VMEM((T, M, R, C), BF16),
+            pltpu.VMEM((T, 8, R), jnp.int32),
+            pltpu.VMEM((1, R + 2 * HALO, 128), jnp.int32),
+            pltpu.VMEM((D, C), BF16),
+            pltpu.VMEM((D, 2 * C), BF16),
+            pltpu.VMEM((M, C, C), BF16),
+            pltpu.VMEM((D, 2 * C), BF16),
+            pltpu.VMEM((M, C, C), BF16),
+            pltpu.VMEM((R, D), BF16),
+            pltpu.VMEM((R, C), BF16),
+            pltpu.VMEM((heads * R, C), BF16),
+            pltpu.VMEM((heads * R, C), BF16),
+            pltpu.VMEM((heads * R, R), F32),
+            pltpu.VMEM((R, heads * R), BF16),
+            pltpu.VMEM((heads, R, 128), F32),
+            pltpu.VMEM((heads, R, 128), F32),
+            pltpu.VMEM((R, C), F32),
+            pltpu.VMEM((R, C), BF16),
+            pltpu.VMEM((R, C), F32),
+            pltpu.VMEM((M, R, C), BF16),
+            pltpu.VMEM((C // 128, R + 2 * HALO, 128), F32),
+            pltpu.VMEM((32, C), F32),
+            part, part, part, part, part, part,
+            dma((11,)),
+            dma((T, M)), dma((2, T)), dma((T,)), dma((T, 2)),
+            dma((T,)), dma((T,)), dma((2,)), dma((2,)), dma((2,)), dma((2,)),
+            dma((2, NCH, 3)), dma((2, NCH, 3)), dma((NCH, 3)), dma((M, NCH)),
+        ],
+        compiler_params=pltpu.CompilerParams(
+            collective_id=0, has_side_effects=True, vmem_limit_bytes=52 * 2**20
+        ),
+    )(
+        tokens, segrow, segcol, ln_att_gain[None, :], w_query, w_keyval.reshape(D, 2 * C),
+        w_out, ln_conv_gain[None, :], w_glu.reshape(D, 2 * C), w_depth, bn_scale[None, :],
+        bn_shift[None, :], w_proj,
+    )
+
+
 def solution(mesh):
     placed = (
         P(("group", "tm"), "mp"),
@@ -155,6 +588,7 @@
         P("mp"),
         P("mp", None),
     )
+    fused = mesh.shape["tm"] == 4 and mesh.shape["mp"] == 4
     return jax.shard_map(
-        per_device, mesh=mesh, in_specs=placed, out_specs=P(("group", "tm"), "mp"), check_vma=False
-    )
+        fused_device if fused else per_device, mesh=mesh, in_specs=placed, out_specs=P(("group", "tm"), "mp"), check_vma=False
+    )

time: 230 us -> 109 us (0.47)
  waiting for transfers between devices: 117 us -> 0 us
  Pallas kernels: 0 us -> 97.9 us
  other arithmetic: 25.4 us -> 0 us
  matrix products: 25 us -> 0 us
  local copies, waits for them, and re-layouts: 27.7 us -> 10.6 us
  between operations: 13.4 us -> 0.04 us
  blocking collectives: 11.9 us -> 0 us
  starting transfers between devices: 6.32 us -> 0 us
    pallas_call x0 -> x1, Pallas kernels: none -> 97.9 us  [fused_device(): pl.pallas_call(functools.partial(block_kernel, T, taps), out_shape=jax.Sh...]
    all_gather x3 -> x0, waiting for transfers between devices: 62.4 us -> none  [the longest x1 32.9 us: per_device(): segment = lax.all_gather(keyval, 'tm', axis=0, tiled=True)]
    unnamed x7 -> x0, waiting for transfers between devices: 52 us -> none
    dot_general x13 -> x0, matrix products: 25 us -> none  [the longest x4 6.41 us: fold_keys(): jnp.einsum('qhd,khd->qhk', query_heads, key_part, preferred_element_type=...]
    reduce_sum x8 -> x0, other arithmetic: 12.7 us -> none  [the longest x4 6.05 us: fold_keys(): weight_sum = weight_sum * factor + jnp.sum(weights, axis=2)]
    all_gather x1 -> x0, blocking collectives: 11.9 us -> none  [per_device(): all_segs = lax.all_gather(segment_ids, 'tm', axis=0, tiled=True)]
    dynamic_slice x13 -> x0, local copies, waits for them, and re-layouts: 8.55 us -> none  [the longest x12 8.47 us: per_device(): result, unused = lax.scan(inner_step, initial, stacked)]
    eq x6 -> x0, other arithmetic: 7.46 us -> none  [the longest x4 5.91 us: fold_keys(): same_seg = (query_segs[:, None] == key_segs[None, :])[:, None, :]]
  transfers between devices with their start and end apart: 7 -> 0, of which waited for: 6 -> 0; matrix products, arithmetic and copies ran while one was open for 5% -> 0% of each run, Pallas kernels for 0% -> 0%
where the time goes in v1:
time: 109 us; the launch traced here: 108 us
  Pallas kernels  97.9 us (90%)
  local copies, waits for them, and re-layouts  10.6 us (10%)
    pallas_call x1, Pallas kernels, fused_device(): pl.pallas_call(functools.partial(block_kernel, T, taps), out_shape=jax.Sh...  97.9 us
    unnamed x11, local copies, waits for them, and re-layouts  6.34 us

profile of v1, /device:TPU:8, one launch (start us, length us, event | category | flops | bytes accessed | tf_op | source)
XLA Modules:
  0.0 108.5 jit_solution(1586114851852498490)
XLA Ops:
  0.0 0.7 broadcast_in_dim.28.bns
  0.7 0.7 broadcast_in_dim.29.bnb
  1.4 0.7 broadcast_in_dim.26.g_att
  2.1 0.7 broadcast_in_dim.27.g_conv
  2.8 0.7 broadcast_in_dim.24.segrow
  3.5 0.8 broadcast_in_dim.25.segcol
  4.2 0.0 copy-start.3
  4.3 3.7 %copy.13 = bf16[192,8,2,384]{3,1,2,0:T(8,128)(2,1)} copy(bf16[192,8,2,384]{3,2,1,0:T(2,128)(2,1)} %bitcast.6) | data formatting | bytes 4718592
  8.0 0.0 copy-done.3
  8.0 0.0 copy-start
  8.0 0.0 copy-start.1
  8.0 0.0 copy-start.2
  8.0 1.9 %copy.14 = bf16[192,8,2,384]{3,1,2,0:T(8,128)(2,1)} copy(bf16[192,8,2,384]{3,2,1,0:T(2,128)(2,1)S(1)} %bitcast.7) | data formatting | bytes 4718592
  9.9 0.0 copy-done
  9.9 0.0 copy-done.1
  9.9 0.0 copy-done.2
  9.9 97.9 %shard_map.118 = bf16[384,384]{1,0:T(8,128)(2,1)S(1)} custom-call(bf16[384,384]{1,0:T(8,128)(2,1)S(1)} %copy-done.1, s32[8,384]{1,0:T(8,128)S(1)} %broadcast_in_dim.24.segrow, s32[384,128]{1,0:T(8,128)S(1)} %broadcast_in_dim.25.segcol, f32[1,1536]{1,0:T(1,128)S(1)} %broadcast_in_dim.26.g_att, bf16[1536,384]{1,0:T(8,128)(2,1)S(1)} %copy-done, ...), custom_call_target="tpu_custom_call" | custom-call | tf_op jit(solution)/shard_map/pallas_call | solution.py:532
  107.8 0.7 copy.16
Async XLA Ops:
  4.2 3.7 %copy-start.3 = (bf16[1536,2,384]{2,1,0:T(2,128)(2,1)S(1)}, bf16[1536,2,384]{2,1,0:T(2,128)(2,1)}, u32[]{:S(2)}) copy-start(bf16[1536,2,384]{2,1,0:T(2,128)(2,1)} %param.19) | copy-start | bytes 7077892
  8.0 1.9 %copy-start = (bf16[1536,384]{1,0:T(8,128)(2,1)S(1)}, bf16[1536,384]{1,0:T(8,128)(2,1)}, u32[]{:S(2)}) copy-start(bf16[1536,384]{1,0:T(8,128)(2,1)} %wq_h.1) | copy-start | bytes 3538948
  8.0 1.9 %copy-start.1 = (bf16[384,384]{1,0:T(8,128)(2,1)S(1)}, bf16[384,384]{1,0:T(8,128)(2,1)}, u32[]{:S(2)}) copy-start(bf16[384,384]{1,0:T(8,128)(2,1)} %tokens.1) | copy-start | bytes 884740
  8.0 1.9 %copy-start.2 = (bf16[31,384]{1,0:T(8,128)(2,1)S(1)}, bf16[31,384]{1,0:T(8,128)(2,1)}, u32[]{:S(2)}) copy-start(bf16[31,384]{1,0:T(8,128)(2,1)} %wdep.1) | copy-start | bytes 71428

commit v2 on v1

--- a/solution.py
+++ b/solution.py
@@ -154,8 +154,8 @@
 
 def block_kernel(
     T, taps,
-    tokens, segrow, segcol, g_att, wq_h, wkv_h, wo_h, g_conv, wg_h, wdep, bns, bnb, wp_h,
-    out,
+    tokens, seg, g_att, wq_h, wkv_h, wo_h, g_conv, wg_h, wdep, bn_s, bn_b, wp_h,
+    out, segcol, gains, bns, bnb,
     tok, seg_all, seg_ext, wq, wkv, wo, wg, wp, nrm, kbuf, qm, vm, sc, pw, mst, lst, acc,
     ctx, keep, mid, ext, wdf, sa, sx, sb, ra, rx, rb,
     wsem, tok_recv, z_send, x_send, m_send, seg_send, seg_recv, hs_send, hs_recv,
@@ -198,8 +198,14 @@
             barrier, inc=1, device_id={"tm": (t + d) % T}, device_id_type=MESH
         )
     tok[t, m] = tokens[...]
-    seg_all[t] = segrow[...]
+    ids = seg[...].reshape(1, R)
+    seg_all[t] = jnp.broadcast_to(ids, (8, R))
+    segcol[...] = jnp.transpose(jnp.broadcast_to(ids, (128, R)))
     seg_ext[0, pl.ds(HALO, R), :] = segcol[...]
+    gains[0] = g_att[...].reshape(1, D)
+    gains[1] = g_conv[...].reshape(1, D)
+    bns[...] = bn_s[...].reshape(1, C)
+    bnb[...] = bn_b[...].reshape(1, C)
     pl.semaphore_wait(barrier, 1 + T)
 
     def z_right(s):
@@ -227,10 +233,10 @@
         def _():
             z_left(s).start()
 
-        over_x(s, m).start()
         to_mate(s, m, 0).start()
 
     launch(t)
+    over_x(t, m).start()
 
     def seg_copy(d):
         return rcopy(seg_all.at[t], seg_all.at[t], seg_send.at[d], seg_recv.at[t],
@@ -249,6 +255,7 @@
 
     has_right = t < T - 1
     has_left = t > 0
+    edge = jnp.logical_or(t == 0, t == T - 1)
 
     @pl.when(has_right)
     def _():
@@ -285,39 +292,54 @@
         inv = lax.rsqrt(jnp.sum(sq, axis=1, keepdims=True) * (1.0 / D) + 1e-05)
         for b in range(M):
             nrm[pl.ds(r0, n), pl.ds(b * C, C)] = (
-                parts[b] * inv * gain[:, pl.ds(b * C, C)]
+                parts[b] * inv * gains[gain, :, pl.ds(b * C, C)]
             ).astype(BF16)
 
     RT = 32
-    coef = float(HEAD_DIM ** (-0.5) * 1.4426950408889634)
+    coef = float(HEAD_DIM ** (-0.5))
+
+    def wide(col):
+        return jnp.concatenate([col] * (C // 128), axis=1)
 
     def softmax_rows(s, rt):
         r0 = pl.multiple_of(rt * RT, RT)
         rows = pl.ds(r0, RT)
-        same = segcol[rows, pl.ds(0, 1)] == seg_all[s, pl.ds(0, 1), :]
-        bias = jnp.where(same, 0.0, NEG)
-        lanes = None
-        for h in range(heads):
-            x = sc[pl.ds(pl.multiple_of(h * R + r0, RT), RT), :] + bias
-            old = mst[h, rows, :]
-            new = jnp.maximum(old, jnp.max(x, axis=1, keepdims=True))
-            f = jnp.exp2((old - new) * coef)
-            p = jnp.exp2((x - new[:, :1]) * coef)
-            lst[h, rows, :] = lst[h, rows, :] * f + jnp.sum(p, axis=1, keepdims=True)
-            mst[h, rows, :] = new
-            pw[rows, pl.ds(h * R, R)] = p.astype(BF16)
-            wide = jnp.broadcast_to(f[:, :1], (RT, C))
-            lanes = wide if lanes is None else jnp.where(head_of == h, wide, lanes)
+        bias = jnp.where(wide(segcol[rows, :]) == seg_all[s, pl.ds(0, 1), :], 0.0, NEG)
+        hs = range(heads)
+        xs = [sc[pl.ds(pl.multiple_of(h * R + r0, RT), RT), :] + bias for h in hs]
+        olds = [mst[h, rows, :] for h in hs]
+        sums = [lst[h, rows, :] for h in hs]
+        news = [jnp.maximum(o, jnp.max(x, axis=1, keepdims=True)) for o, x in zip(olds, xs)]
+        fs = [jnp.exp((o - n) * coef) for o, n in zip(olds, news)]
+        ps = [jnp.exp((x - wide(n)) * coef) for x, n in zip(xs, news)]
+        sums = [v * f + jnp.sum(p, axis=1, keepdims=True) for v, f, p in zip(sums, fs, ps)]
+        lanes = wide(fs[0])
+        for h in hs[1:]:
+            lanes = jnp.where(head_of == h, wide(fs[h]), lanes)
+        for h in hs:
+            mst[h, rows, :] = news[h]
+            lst[h, rows, :] = sums[h]
+            pw[rows, pl.ds(h * R, R)] = ps[h].astype(BF16)
         acc[rows, :] = acc[rows, :] * lanes
 
     def block_step(i, code):
         s = code % T
         nxt = (code // T) % T
-
-        @pl.when(i + 1 < T)
+        after = (code // (T * T)) % T
+
+        @pl.when(jnp.logical_or(i == 0, jnp.logical_and(edge, i + 1 < T)))
         def _():
             z_right(nxt).wait_recv()
             launch(nxt)
+
+        @pl.when(jnp.logical_and(jnp.logical_not(edge), i < 2))
+        def _():
+            z_right(after).wait_recv()
+            launch(after)
+
+        @pl.when(i + 1 < T)
+        def _():
+            over_x(nxt, m).start()
 
         over_x(s, cross).wait_recv()
         to_mate(s, cross, 1).start()
@@ -336,7 +358,7 @@
 
         @pl.loop(0, R // RT)
         def _(rt):
-            norm_rows(lambda b, r0, n: tok[s, b, pl.ds(r0, n), :], g_att,
+            norm_rows(lambda b, r0, n: tok[s, b, pl.ds(r0, n), :], 0,
                       pl.multiple_of(rt * RT, RT), RT)
 
         @pl.when(i == 0)
@@ -367,8 +389,8 @@
 
     den = None
     for h in range(heads):
-        wide = jnp.broadcast_to(lst[h, :, pl.ds(0, 1)], (R, C))
-        den = wide if den is None else jnp.where(head_of == h, wide, den)
+        col = wide(lst[h, :, :])
+        den = col if den is None else jnp.where(head_of == h, col, den)
     ctx[...] = (acc[...] / den).astype(BF16)
 
     def rs_a(ph, ch):
@@ -425,7 +447,7 @@
 
         @pl.loop(0, CR // RT)
         def _(rt):
-            norm_rows(lambda b, r0, n: mid[b, pl.ds(r0, n), :], g_conv,
+            norm_rows(lambda b, r0, n: mid[b, pl.ds(r0, n), :], 1,
                       pl.multiple_of(ch * CR + rt * RT, RT), RT)
 
         a = nrm[rows, :]
@@ -523,8 +545,6 @@
     heads = C // HEAD_DIM
     taps = w_depth.shape[0]
     CR = R // NCH
-    segrow = jnp.broadcast_to(segment_ids[None, :], (8, R))
-    segcol = jnp.broadcast_to(segment_ids[:, None], (R, 128))
     vmem = pl.BlockSpec(memory_space=pltpu.VMEM)
     hbm = pl.BlockSpec(memory_space=pl.ANY)
     dma = pltpu.SemaphoreType.DMA
@@ -532,9 +552,13 @@
     return pl.pallas_call(
         functools.partial(block_kernel, T, taps),
         out_shape=jax.ShapeDtypeStruct((R, C), BF16),
-        in_specs=[vmem, vmem, vmem, vmem, hbm, hbm, hbm, vmem, hbm, vmem, vmem, vmem, hbm],
+        in_specs=[vmem, vmem, vmem, hbm, hbm, hbm, vmem, hbm, vmem, vmem, vmem, hbm],
         out_specs=vmem,
         scratch_shapes=[
+            pltpu.VMEM((R, 128), jnp.int32),
+            pltpu.VMEM((2, 1, D), F32),
+            pltpu.VMEM((1, C), F32),
+            pltpu.VMEM((1, C), F32),
             pltpu.VMEM((T, M, R, C), BF16),
             pltpu.VMEM((T, 8, R), jnp.int32),
             pltpu.VMEM((1, R + 2 * HALO, 128), jnp.int32),
@@ -567,9 +591,8 @@
             collective_id=0, has_side_effects=True, vmem_limit_bytes=52 * 2**20
         ),
     )(
-        tokens, segrow, segcol, ln_att_gain[None, :], w_query, w_keyval.reshape(D, 2 * C),
-        w_out, ln_conv_gain[None, :], w_glu.reshape(D, 2 * C), w_depth, bn_scale[None, :],
-        bn_shift[None, :], w_proj,
+        tokens, segment_ids, ln_att_gain, w_query, w_keyval.reshape(D, 2 * C),
+        w_out, ln_conv_gain, w_glu.reshape(D, 2 * C), w_depth, bn_scale, bn_shift, w_proj,
     )
 
 

time: 109 us -> 91.8 us (0.84)
  Pallas kernels: 97.9 us -> 85.2 us
  local copies, waits for them, and re-layouts: 10.6 us -> 6.37 us
    pallas_call x1, Pallas kernels: 97.9 us -> 85.2 us  [fused_device(): pl.pallas_call(functools.partial(block_kernel, T, taps), out_shape=jax.Sh...]
    broadcast_in_dim x6 -> x0, local copies, waits for them, and re-layouts: 4.23 us -> none  [the longest x1 0.78 us: fused_device(): segcol = jnp.broadcast_to(segment_ids[:, None], (R, 128))]
    unnamed x11 -> x21, local copies, waits for them, and re-layouts: 6.34 us -> 6.37 us
where the time goes in v2:
time: 91.8 us; the launch traced here: 91.7 us
  Pallas kernels  85.2 us (93%)
  local copies, waits for them, and re-layouts  6.37 us (7%)
    pallas_call x1, Pallas kernels, fused_device(): pl.pallas_call(functools.partial(block_kernel, T, taps), out_shape=jax.Sh...  85.2 us
    unnamed x21, local copies, waits for them, and re-layouts  6.37 us

profile of v2, /device:TPU:8, one launch (start us, length us, event | category | flops | bytes accessed | tf_op | source)
XLA Modules:
  0.0 91.7 jit_solution(5088093597109325817)
XLA Ops:
  0.0 0.0 copy-start.8
  0.0 3.7 %copy.13 = bf16[192,8,2,384]{3,1,2,0:T(8,128)(2,1)} copy(bf16[192,8,2,384]{3,2,1,0:T(2,128)(2,1)} %bitcast.6) | data formatting | bytes 4718592
  3.7 0.0 copy-done.8
  3.7 0.0 copy-start
  3.7 0.0 copy-start.1
  3.7 0.0 copy-start.2
  3.7 0.0 copy-start.3
  3.7 0.0 copy-start.4
  3.7 0.0 copy-start.5
  3.8 0.0 copy-start.6
  3.8 0.0 copy-start.7
  3.8 1.9 %copy.14 = bf16[192,8,2,384]{3,1,2,0:T(8,128)(2,1)} copy(bf16[192,8,2,384]{3,2,1,0:T(2,128)(2,1)S(1)} %bitcast.7) | data formatting | bytes 4718592
  5.7 0.0 copy-done
  5.7 0.0 copy-done.1
  5.7 0.0 copy-done.2
  5.7 0.0 copy-done.3
  5.7 0.0 copy-done.4
  5.7 0.0 copy-done.5
  5.7 0.0 copy-done.6
  5.7 0.0 copy-done.7
  5.7 85.2 %shard_map.118 = bf16[384,384]{1,0:T(8,128)(2,1)S(1)} custom-call(bf16[384,384]{1,0:T(8,128)(2,1)S(1)} %copy-done.1, s32[384]{0:T(512)S(1)} %copy-done.5, f32[1536]{0:T(1024)S(1)} %copy-done.3, bf16[1536,384]{1,0:T(8,128)(2,1)S(1)} %copy-done, bf16[1536,768]{1,0:T(8,128)(2,1)} %bitcast.4, bf16[384,1536]{1,0:T(8,128)(2,1)} %wo_h.1, f32[1536]{0:T(1024)S(1)} %copy-done.4, ...), custom_call_target="tpu_custom_call" | custom-call | tf_op jit(solution)/shard_map/pallas_call | solution.py:552
  91.0 0.7 copy.16
Async XLA Ops:
  0.0 3.7 %copy-start.8 = (bf16[1536,2,384]{2,1,0:T(2,128)(2,1)S(1)}, bf16[1536,2,384]{2,1,0:T(2,128)(2,1)}, u32[]{:S(2)}) copy-start(bf16[1536,2,384]{2,1,0:T(2,128)(2,1)} %param.19) | copy-start | bytes 7077892
  3.7 2.0 %copy-start = (bf16[1536,384]{1,0:T(8,128)(2,1)S(1)}, bf16[1536,384]{1,0:T(8,128)(2,1)}, u32[]{:S(2)}) copy-start(bf16[1536,384]{1,0:T(8,128)(2,1)} %wq_h.1) | copy-start | bytes 3538948
  3.7 2.0 %copy-start.1 = (bf16[384,384]{1,0:T(8,128)(2,1)S(1)}, bf16[384,384]{1,0:T(8,128)(2,1)}, u32[]{:S(2)}) copy-start(bf16[384,384]{1,0:T(8,128)(2,1)} %tokens.1) | copy-start | bytes 884740
  3.7 2.0 %copy-start.2 = (bf16[31,384]{1,0:T(8,128)(2,1)S(1)}, bf16[31,384]{1,0:T(8,128)(2,1)}, u32[]{:S(2)}) copy-start(bf16[31,384]{1,0:T(8,128)(2,1)} %wdep.1) | copy-start | bytes 71428
  3.7 2.0 %copy-start.3 = (f32[1536]{0:T(1024)S(1)}, f32[1536]{0:T(1024)}, u32[]{:S(2)}) copy-start(f32[1536]{0:T(1024)} %g_att.1) | copy-start | bytes 18436
  3.7 2.0 %copy-start.4 = (f32[1536]{0:T(1024)S(1)}, f32[1536]{0:T(1024)}, u32[]{:S(2)}) copy-start(f32[1536]{0:T(1024)} %g_conv.1) | copy-start | bytes 18436
  3.7 2.0 %copy-start.5 = (s32[384]{0:T(512)S(1)}, s32[384]{0:T(512)}, u32[]{:S(2)}) copy-start(s32[384]{0:T(512)} %seg.1) | copy-start | bytes 4612
  3.8 2.0 %copy-start.6 = (f32[384]{0:T(512)S(1)}, f32[384]{0:T(512)}, u32[]{:S(2)}) copy-start(f32[384]{0:T(512)} %bn_s.1) | copy-start | bytes 4612
  3.8 2.0 %copy-start.7 = (f32[384]{0:T(512)S(1)}, f32[384]{0:T(512)}, u32[]{:S(2)}) copy-start(f32[384]{0:T(512)} %bn_b.1) | copy-start | bytes 4612

commit v3 on v2

--- a/solution.py
+++ b/solution.py
@@ -147,6 +147,8 @@
 NEG = -1e30
 HALO = 16
 NCH = 2
+RS = 128
+RN = 96
 MESH = pl.DeviceIdType.MESH
 F32 = jnp.float32
 BF16 = jnp.bfloat16
@@ -298,21 +300,24 @@
     RT = 32
     coef = float(HEAD_DIM ** (-0.5))
 
+    def fold(x):
+        return sum(x[:, k * 128:(k + 1) * 128] for k in range(1, C // 128)) + x[:, :128]
+
     def wide(col):
         return jnp.concatenate([col] * (C // 128), axis=1)
 
     def softmax_rows(s, rt):
-        r0 = pl.multiple_of(rt * RT, RT)
-        rows = pl.ds(r0, RT)
+        r0 = pl.multiple_of(rt * RS, RS)
+        rows = pl.ds(r0, RS)
         bias = jnp.where(wide(segcol[rows, :]) == seg_all[s, pl.ds(0, 1), :], 0.0, NEG)
         hs = range(heads)
-        xs = [sc[pl.ds(pl.multiple_of(h * R + r0, RT), RT), :] + bias for h in hs]
+        xs = [sc[pl.ds(pl.multiple_of(h * R + r0, RS), RS), :] + bias for h in hs]
         olds = [mst[h, rows, :] for h in hs]
         sums = [lst[h, rows, :] for h in hs]
         news = [jnp.maximum(o, jnp.max(x, axis=1, keepdims=True)) for o, x in zip(olds, xs)]
         fs = [jnp.exp((o - n) * coef) for o, n in zip(olds, news)]
         ps = [jnp.exp((x - wide(n)) * coef) for x, n in zip(xs, news)]
-        sums = [v * f + jnp.sum(p, axis=1, keepdims=True) for v, f, p in zip(sums, fs, ps)]
+        sums = [v * f + fold(p) for v, f, p in zip(sums, fs, ps)]
         lanes = wide(fs[0])
         for h in hs[1:]:
             lanes = jnp.where(head_of == h, wide(fs[h]), lanes)
@@ -356,10 +361,10 @@
             rcopy(seg_all.at[s], seg_all.at[s], seg_send.at[0], seg_recv.at[s],
                   tm=(t + 1) % T).wait_recv()
 
-        @pl.loop(0, R // RT)
+        @pl.loop(0, R // RN)
         def _(rt):
             norm_rows(lambda b, r0, n: tok[s, b, pl.ds(r0, n), :], 0,
-                      pl.multiple_of(rt * RT, RT), RT)
+                      pl.multiple_of(rt * RN, RN), RN)
 
         @pl.when(i == 0)
         def _():
@@ -377,7 +382,7 @@
                 qm[pl.ds(h * R, R), :], kbuf[...], (((1,), (1,)), ((), ())),
                 preferred_element_type=F32)
 
-        @pl.loop(0, R // RT)
+        @pl.loop(0, R // RS)
         def _(rt):
             softmax_rows(s, rt)
 
@@ -389,7 +394,7 @@
 
     den = None
     for h in range(heads):
-        col = wide(lst[h, :, :])
+        col = jnp.sum(lst[h, :, :], axis=1, keepdims=True)
         den = col if den is None else jnp.where(head_of == h, col, den)
     ctx[...] = (acc[...] / den).astype(BF16)
 
@@ -445,10 +450,10 @@
         mid_copy(mate, ch, 1, mp=mate).wait_recv()
         mid_copy(diag, ch, 2, mp=mate).wait_recv()
 
-        @pl.loop(0, CR // RT)
+        @pl.loop(0, CR // RN)
         def _(rt):
             norm_rows(lambda b, r0, n: mid[b, pl.ds(r0, n), :], 1,
-                      pl.multiple_of(ch * CR + rt * RT, RT), RT)
+                      pl.multiple_of(ch * CR + rt * RN, RN), RN)
 
         a = nrm[rows, :]
         val = jnp.dot(a, wg[:, pl.ds(0, C)], preferred_element_type=F32)

time: 91.8 us -> 81.5 us (0.89)
  Pallas kernels: 85.2 us -> 74.9 us
    pallas_call x1, Pallas kernels: 85.2 us -> 74.9 us  [fused_device(): pl.pallas_call(functools.partial(block_kernel, T, taps), out_shape=jax.Sh...]
where the time goes in v3:
time: 81.5 us; the launch traced here: 81.4 us
  Pallas kernels  74.9 us (92%)
  local copies, waits for them, and re-layouts  6.37 us (8%)
    pallas_call x1, Pallas kernels, fused_device(): pl.pallas_call(functools.partial(block_kernel, T, taps), out_shape=jax.Sh...  74.9 us
    unnamed x21, local copies, waits for them, and re-layouts  6.37 us

profile of v3, /device:TPU:8, one launch (start us, length us, event | category | flops | bytes accessed | tf_op | source)
XLA Modules:
  0.0 81.4 jit_solution(7989780674155447727)
XLA Ops:
  0.0 0.0 copy-start.8
  0.0 3.7 %copy.13 = bf16[192,8,2,384]{3,1,2,0:T(8,128)(2,1)} copy(bf16[192,8,2,384]{3,2,1,0:T(2,128)(2,1)} %bitcast.6) | data formatting | bytes 4718592
  3.7 0.0 copy-done.8
  3.7 0.0 copy-start
  3.7 0.0 copy-start.1
  3.7 0.0 copy-start.2
  3.7 0.0 copy-start.3
  3.7 0.0 copy-start.4
  3.7 0.0 copy-start.5
  3.8 0.0 copy-start.6
  3.8 0.0 copy-start.7
  3.8 1.9 %copy.14 = bf16[192,8,2,384]{3,1,2,0:T(8,128)(2,1)} copy(bf16[192,8,2,384]{3,2,1,0:T(2,128)(2,1)S(1)} %bitcast.7) | data formatting | bytes 4718592
  5.7 0.0 copy-done
  5.7 0.0 copy-done.1
  5.7 0.0 copy-done.2
  5.7 0.0 copy-done.3
  5.7 0.0 copy-done.4
  5.7 0.0 copy-done.5
  5.7 0.0 copy-done.6
  5.7 0.0 copy-done.7
  5.7 74.9 %shard_map.118 = bf16[384,384]{1,0:T(8,128)(2,1)S(1)} custom-call(bf16[384,384]{1,0:T(8,128)(2,1)S(1)} %copy-done.1, s32[384]{0:T(512)S(1)} %copy-done.5, f32[1536]{0:T(1024)S(1)} %copy-done.3, bf16[1536,384]{1,0:T(8,128)(2,1)S(1)} %copy-done, bf16[1536,768]{1,0:T(8,128)(2,1)} %bitcast.4, bf16[384,1536]{1,0:T(8,128)(2,1)} %wo_h.1, f32[1536]{0:T(1024)S(1)} %copy-done.4, ...), custom_call_target="tpu_custom_call" | custom-call | tf_op jit(solution)/shard_map/pallas_call | solution.py:557
  80.7 0.7 copy.16
Async XLA Ops:
  0.0 3.7 %copy-start.8 = (bf16[1536,2,384]{2,1,0:T(2,128)(2,1)S(1)}, bf16[1536,2,384]{2,1,0:T(2,128)(2,1)}, u32[]{:S(2)}) copy-start(bf16[1536,2,384]{2,1,0:T(2,128)(2,1)} %param.19) | copy-start | bytes 7077892
  3.7 2.0 %copy-start = (bf16[1536,384]{1,0:T(8,128)(2,1)S(1)}, bf16[1536,384]{1,0:T(8,128)(2,1)}, u32[]{:S(2)}) copy-start(bf16[1536,384]{1,0:T(8,128)(2,1)} %wq_h.1) | copy-start | bytes 3538948
  3.7 2.0 %copy-start.1 = (bf16[384,384]{1,0:T(8,128)(2,1)S(1)}, bf16[384,384]{1,0:T(8,128)(2,1)}, u32[]{:S(2)}) copy-start(bf16[384,384]{1,0:T(8,128)(2,1)} %tokens.1) | copy-start | bytes 884740
  3.7 2.0 %copy-start.2 = (bf16[31,384]{1,0:T(8,128)(2,1)S(1)}, bf16[31,384]{1,0:T(8,128)(2,1)}, u32[]{:S(2)}) copy-start(bf16[31,384]{1,0:T(8,128)(2,1)} %wdep.1) | copy-start | bytes 71428
  3.7 2.0 %copy-start.3 = (f32[1536]{0:T(1024)S(1)}, f32[1536]{0:T(1024)}, u32[]{:S(2)}) copy-start(f32[1536]{0:T(1024)} %g_att.1) | copy-start | bytes 18436
  3.7 2.0 %copy-start.4 = (f32[1536]{0:T(1024)S(1)}, f32[1536]{0:T(1024)}, u32[]{:S(2)}) copy-start(f32[1536]{0:T(1024)} %g_conv.1) | copy-start | bytes 18436
  3.7 2.0 %copy-start.5 = (s32[384]{0:T(512)S(1)}, s32[384]{0:T(512)}, u32[]{:S(2)}) copy-start(s32[384]{0:T(512)} %seg.1) | copy-start | bytes 4612
  3.8 2.0 %copy-start.6 = (f32[384]{0:T(512)S(1)}, f32[384]{0:T(512)}, u32[]{:S(2)}) copy-start(f32[384]{0:T(512)} %bn_s.1) | copy-start | bytes 4612
  3.8 2.0 %copy-start.7 = (f32[384]{0:T(512)S(1)}, f32[384]{0:T(512)}, u32[]{:S(2)}) copy-start(f32[384]{0:T(512)} %bn_b.1) | copy-start | bytes 4612
